TPU v7x, 32 devices: a whole 2x2x4 slice. The times are simulated.
32 devices in a mesh: dp: 4 (over y, core), seq: 8 (over z, x).
Axes of the slice: x: 2, y: 2, z: 4, core: 2. Of those that a mesh axis runs over, the one named last changes fastest.
Arguments:
- tokens: bfloat16 [4, 24, 256, 1280], P('dp', 'seq'), may hold values from -6 to 6
- clip_ids: int32 [4, 24], P('dp'), may hold values from 0 to 5, never falling along the last dimension, each value on 1 to 12 neighbouring positions
- ln_gain: float32 [1280], replicated, may hold values from 0.1 to 1.9
- w_qkv: bfloat16 [1280, 1920], P(None, 'dp'), may hold values from -0.15625 to 0.15625
- w_out: bfloat16 [640, 1280], P(None, 'dp'), may hold values from -0.25 to 0.25
Outputs:
- output: bfloat16 [4, 24, 256, 1280], P('dp', 'seq')
Inputs may be any that keep to these rules, and one draw needn't show every extreme that they name: `clip_ids`: in each batch the clip numbers never fall along the frames, every clip number occurs, each clip covers 1 to 12 consecutive frames, and some clip covers exactly 12.
All inputs are finite; a program needn't handle non-finite values.
Results may differ from a plain program's by a relative error of at most 0.006.
Values may be sent and summed in bfloat16 or wider, within the bound.
A program may use at most 64 MiB of HBM per device.

v0:
```python
import math
import jax
import jax.numpy as jnp
from jax import lax
from jax.sharding import PartitionSpec as P

HS = 80
HEADS = 8
HD = 640
norm_eps = 1e-05


def layer_norm(block, ln_gain):
    values = block.astype(jnp.float32)
    center = jnp.mean(values, axis=-1, keepdims=True)
    spread = jnp.mean(jnp.square(values - center), axis=-1, keepdims=True)
    return ((values - center) * lax.rsqrt(spread + norm_eps) * ln_gain).astype(jnp.bfloat16)


def split_heads(projected):
    queries = (projected[:, :HD] * (1.0 / math.sqrt(HS))).astype(jnp.bfloat16)
    keys = projected[:, HD : 2 * HD].astype(jnp.bfloat16)
    values = projected[:, 2 * HD :].astype(jnp.bfloat16)
    return (queries, keys, values)


def attend(queries, keys, values, clip_row):
    scores = jnp.einsum("flhe,glhe->lhfg", queries, keys, preferred_element_type=jnp.float32)
    same_clip = clip_row[:, None] == clip_row[None, :]
    raised = jnp.where(same_clip, jnp.exp(scores), jnp.zeros_like(scores))
    attn_probs = (raised / jnp.sum(raised, axis=-1, keepdims=True)).astype(jnp.bfloat16)
    return jnp.einsum(
        "lhfg,glhe->flhe", attn_probs, values, preferred_element_type=jnp.float32
    ).astype(jnp.bfloat16)


def shards(tokens, clip_ids, ln_gain, w_qkv, w_out):
    width = tokens.shape[3]
    clip_row = clip_ids[0]
    frames = clip_row.shape[0]
    local_frames = tokens.shape[1]
    patches = tokens.shape[2]
    moved = lax.all_to_all(tokens, "seq", split_axis=2, concat_axis=1, tiled=True)
    places = moved.shape[2]
    normed = layer_norm(moved, ln_gain).reshape(frames * places, width)

    def column_block(piece, start):
        return jnp.dot(normed, piece, preferred_element_type=jnp.float32)

    queries, keys, values = split_heads(
        column_block(lax.all_gather(w_qkv, "dp", axis=1, tiled=True), jnp.int32(0))
    )
    head_shape = (frames, places, HEADS, HS)
    mixed = attend(
        queries.reshape(head_shape), keys.reshape(head_shape), values.reshape(head_shape), clip_row
    )
    mixed = lax.all_to_all(
        mixed.reshape(1, frames, places, HD), "seq", split_axis=1, concat_axis=2, tiled=True
    )
    row_count = local_frames * patches
    rows_in = mixed.reshape(row_count, HD)

    def column_block(piece, start):
        return jnp.dot(rows_in, piece, preferred_element_type=jnp.float32)

    update = column_block(lax.all_gather(w_out, "dp", axis=1, tiled=True), jnp.int32(0))
    summed = tokens.reshape(row_count, width).astype(jnp.float32) + update
    return summed.astype(jnp.bfloat16).reshape(tokens.shape)


def solution(mesh):
    placed = (P("dp", "seq", None, None), P("dp", None), P(), P(None, "dp"), P(None, "dp"))
    return jax.shard_map(
        shards, mesh=mesh, in_specs=placed, out_specs=P("dp", "seq", None, None), check_vma=False
    )
```

profile of v0, /device:TPU:0, one launch (start us, length us, event | category | flops | bytes accessed | tf_op | source)
XLA Modules:
  0.0 151.9 jit_solution(18149255715372341711)
XLA Ops:
  6.5 0.0 all-gather.3.cloned.1.call-start
  6.5 0.7 all-gather.3.cloned.1.call-update
  7.3 4.8 %copy.35 = bf16[1,3,256,1280]{3,1,0,2:T(4,128)(2,1)} copy(bf16[1,3,256,1280]{3,2,1,0:T(8,128)(2,1)} %param.5) | data formatting | bytes 3932160 | tf_op args[0]
  12.0 7.4 %all-to-all-start = ((bf16[1,3,256,1280]{3,1,0,2:T(4,128)(2,1)}), bf16[1,3,256,1280]{3,1,0,2:T(4,128)(2,1)S(1)}, u32[]{:S(2)}, u32[]{:S(2)}) async-start(bf16[1,3,256,1280]{3,1,0,2:T(4,128)(2,1)} %copy.35), calls=%async_computation | async-start | bytes 5242880 | tf_op jit(solution)/shard_map/all_to_all | solution.py:43
  19.4 0.0 all-gather.5.cloned.1.call-start
  19.5 0.7 all-gather.5.cloned.1.call-update
  20.2 0.0 copy-done.2
  20.2 0.1 broadcast_compare_fusion
  20.3 58.6 %all-to-all-done = bf16[1,3,256,1280]{3,1,0,2:T(4,128)(2,1)S(1)} async-done(((bf16[1,3,256,1280]{3,1,0,2:T(4,128)(2,1)}), bf16[1,3,256,1280]{3,1,0,2:T(4,128)(2,1)S(1)}, u32[]{:S(2)}, u32[]{:S(2)}) %all-to-all-start) | async-done | bytes 1966112 | tf_op jit(solution)/shard_map/all_to_all | solution.py:43
  78.9 2.3 %convert_bitcast_fusion = (f32[1,8,3,32,1280]{4,3,1,2,0:T(8,128)}, bf16[1,3,256,1280]{3,2,1,0:T(8,128)(2,1)S(1)}) fusion(bf16[1,3,256,1280]{3,1,0,2:T(4,128)(2,1)S(1)} %all-to-all-done), kind=kLoop, calls=%fused_computation.1 | loop fusion | flops 983040 | bytes 7864320 | tf_op jit(solution)/shard_map/convert_element_type | solution.py:14
  81.2 0.3 fusion.5
  81.6 0.7 multiply_reduce_fusion
  82.3 0.1 rsqrt.12
  82.4 0.1 div.17
  82.4 2.4 %copy.37 = f32[1,8,3,32,1280]{4,3,2,1,0:T(8,128)S(1)} copy(f32[1,8,3,32,1280]{4,3,1,2,0:T(8,128)} %get-tuple-element.5) | data formatting | bytes 7864320 | tf_op jit(solution)/shard_map/convert_element_type | solution.py:14
  84.9 0.6 fusion.2
  85.4 0.0 all-gather.3.cloned.1.call-done
  85.5 8.5 %fusion.18 = (bf16[768,1920]{1,0:T(8,128)(2,1)S(1)}, f32[768,1920]{1,0:T(8,128)}) fusion(bf16[768,1280]{1,0:T(8,128)(2,1)S(1)} %fusion.2, bf16[1280,1920]{0,1:T(8,128)(2,1)} %all-gather.3.cloned.1.call-done), kind=kOutput, calls=%fused_computation.27 | convolution fusion | flops 3776348160 | bytes 15728640 | tf_op jit(solution)/shard_map/dot_general | solution.py:48
  94.0 0.2 fusion.17
  94.2 1.6 %reshape.90 = bf16[24,32,8,80]{3,2,1,0:T(8,128)(2,1)S(1)} reshape(bf16[768,640]{1,0:T(8,128)(2,1)S(1)} %get-tuple-element.8) | data formatting | bytes 1966080 | tf_op jit(solution)/shard_map/reshape | solution.py:55
  95.8 1.7 %fusion.6 = bf16[768,640]{1,0:T(8,128)(2,1)S(1)} fusion(f32[768,1920]{1,0:T(8,128)} %get-tuple-element.10), kind=kLoop, calls=%fused_computation.13 | loop fusion | flops 983040 | bytes 2949120 | tf_op jit(solution)/shard_map/convert_element_type | solution.py:21
  97.5 2.5 %reshape.89 = bf16[24,32,8,80]{3,2,1,0:T(8,128)(2,1)} reshape(bf16[768,640]{1,0:T(8,128)(2,1)S(1)} %fusion.6) | data formatting | bytes 1966080 | tf_op jit(solution)/shard_map/reshape | solution.py:55
  100.0 5.7 %fusion.4 = (f32[32,8,24]{2,1,0:T(8,128)S(1)}, f32[32,8,24,24]{2,3,1,0:T(8,128)}) fusion(pred[24,24]{0,1:T(8,128)(4,1)S(1)} %broadcast_compare_fusion, bf16[24,32,8,80]{3,2,1,0:T(8,128)(2,1)S(1)} %reshape.90, bf16[24,32,8,80]{3,2,1,0:T(8,128)(2,1)} %reshape.89), kind=kOutput, calls=%fused_computation.10 | convolution fusion | flops 23881728 | bytes 2581056 | tf_op jit(solution)/shard_map/flhe,glhe->lhfg/dot_general | solution.py:28
  105.7 1.6 %reshape.88 = bf16[24,32,8,80]{3,2,1,0:T(8,128)(2,1)S(1)} reshape(bf16[768,640]{1,0:T(8,128)(2,1)S(1)} %get-tuple-element.7) | data formatting | bytes 1966080 | tf_op jit(solution)/shard_map/reshape | solution.py:55
  107.3 3.4 %fusion.13 = bf16[24,32,8,80]{3,0,2,1:T(8,128)(2,1)S(1)} fusion(f32[32,8,24,24]{2,3,1,0:T(8,128)} %get-tuple-element.12, f32[32,8,24]{2,1,0:T(8,128)S(1)} %get-tuple-element.11, pred[24,24]{0,1:T(8,128)(4,1)S(1)} %broadcast_compare_fusion, bf16[24,32,8,80]{3,2,1,0:T(8,128)(2,1)S(1)} %reshape.88), kind=kOutput, calls=%fused_computation.21 | convolution fusion | flops 24526848 | bytes 2581056 | tf_op jit(solution)/shard_map/lhfg,glhe->flhe/dot_general | solution.py:32
  110.7 0.3 copy.44
  111.1 1.2 reshape.91
  112.3 0.0 copy-start
  112.3 28.2 %all_to_all.24 = bf16[1,24,32,640]{3,2,0,1:T(8,128)(2,1)S(1)} all-to-all(bf16[1,24,32,640]{3,2,0,1:T(8,128)(2,1)S(1)} %bitcast.36), channel_id=1, replica_groups=mesh['dp'=4,'seq'=8] {'seq'}, dimensions={1} | all-to-all | bytes 1966080 | tf_op jit(solution)/shard_map/all_to_all | solution.py:57
  140.5 0.1 copy.46
  140.6 0.0 all-gather.5.cloned.1.call-done
  140.6 4.4 %fusion.3 = bf16[768,1280]{1,0:T(8,128)(2,1)} fusion(bf16[768,640]{1,0:T(8,128)(2,1)S(1)} %bitcast.39, bf16[640,1280]{0,1:T(8,128)(2,1)} %all-gather.5.cloned.1.call-done, bf16[768,1280]{1,0:T(8,128)(2,1)S(1)} %bitcast.38), kind=kOutput, calls=%fused_computation.7 | convolution fusion | flops 1261240320 | bytes 6553600 | tf_op jit(solution)/shard_map/dot_general | solution.py:64
  (8 shorter events, 0.0 us)
Async XLA Ops:
  6.5 78.9 %all-gather.3.cloned.1.call-start = ((), (), s32[]{:S(2)}) async-start(), calls=%async_computation.2 | async-start | bytes 6144000 | tf_op jit(solution)/shard_map/all_gather | solution.py:51
  12.0 8.2 %copy-start.2 = (s32[1,24]{1,0:T(1,128)S(1)}, s32[1,24]{1,0:T(1,128)}, u32[]{:S(2)}) copy-start(s32[1,24]{1,0:T(1,128)} %param.6) | copy-start | bytes 292
  12.0 66.9 %all-to-all-start = ((bf16[1,3,256,1280]{3,1,0,2:T(4,128)(2,1)}), bf16[1,3,256,1280]{3,1,0,2:T(4,128)(2,1)S(1)}, u32[]{:S(2)}, u32[]{:S(2)}) async-start(bf16[1,3,256,1280]{3,1,0,2:T(4,128)(2,1)} %copy.35), calls=%async_computation | async-start | bytes 5242880 | tf_op jit(solution)/shard_map/all_to_all | solution.py:43
  19.4 121.2 %all-gather.5.cloned.1.call-start = ((), (), s32[]{:S(2)}) async-start(), calls=%async_computation.3 | async-start | bytes 2048000 | tf_op jit(solution)/shard_map/all_gather | solution.py:66
  82.4 2.4 %copy-start.1 = (f32[1280]{0:T(1024)S(1)}, f32[1280]{0:T(1024)}, u32[]{:S(2)}) copy-start(f32[1280]{0:T(1024)} %param.7) | copy-start | bytes 15364
  112.3 28.3 %copy-start = (bf16[1,3,256,1280]{3,2,1,0:T(8,128)(2,1)S(1)}, bf16[1,3,256,1280]{3,2,1,0:T(8,128)(2,1)}, u32[]{:S(2)}) copy-start(bf16[1,3,256,1280]{3,2,1,0:T(8,128)(2,1)} %param.5) | copy-start | bytes 5898244
Sparse Core Ops, SparseCore 0:
  8.9 41.2 all-gather.2
  51.8 19.9 all-gather.4
where the time goes:
time: 152 us
  waiting for transfers between devices  60.1 us (40%)
  blocking collectives  28.2 us (19%)
  matrix products  22 us (14%)
  local copies, waits for them, and re-layouts  14.9 us (10%)
  between operations  13.6 us (9%)
  starting transfers between devices  7.45 us (5%)
  other arithmetic  5.69 us (4%)
    all_to_all x1, waiting for transfers between devices, shards(): lax.all_to_all(tokens, 'seq', split_axis=2, concat_axis=1, tiled=True)  58.6 us
    all_to_all x1, blocking collectives, shards(): lax.all_to_all(mixed.reshape(1, frames, places, HD), 'seq', split_axis=1,...  28.2 us
    dot_general x1, matrix products, column_block(): return jnp.dot(normed, piece, preferred_element_type=jnp.float32)  8.52 us
    all_to_all x1, starting transfers between devices, shards(): lax.all_to_all(tokens, 'seq', split_axis=2, concat_axis=1, tiled=True)  7.41 us
    dot_general x1, matrix products, attend(): jnp.einsum('flhe,glhe->lhfg', queries, keys, preferred_element_type=jnp.f...  5.69 us
    unnamed x7, local copies, waits for them, and re-layouts  4.77 us
    dot_general x1, matrix products, column_block(): return jnp.dot(rows_in, piece, preferred_element_type=jnp.float32)  4.43 us
    dot_general x1, matrix products, attend(): jnp.einsum('lhfg,glhe->flhe', attn_probs, values, preferred_element_type=...  3.4 us
  transfers between devices with their start and end apart: 3, of which 1 were waited for; matrix products, arithmetic and copies ran while one was open for 25% of the time, Pallas kernels for 0%

commit v1 on v0

--- a/solution.py
+++ b/solution.py
@@ -40,7 +40,30 @@
     frames = clip_row.shape[0]
     local_frames = tokens.shape[1]
     patches = tokens.shape[2]
-    moved = lax.all_to_all(tokens, "seq", split_axis=2, concat_axis=1, tiled=True)
+
+    def spread_plane_on(unit):
+        axis_id = "seq"
+        z1 = lax.axis_size(axis_id)
+        finding = lax.axis_index(axis_id)
+        view_out, right_arr = (z1, finding)
+        local_next = unit.shape[2] // view_out
+        mid_arr = list(unit.shape)
+        mid_arr[2] = local_next
+        tile_out = mid_arr[1]
+        mid_arr[1] = tile_out * view_out
+        z2 = jnp.zeros(mid_arr, unit.dtype)
+        for nth in range(view_out):
+            k_now = lax.dynamic_slice_in_dim(
+                unit, (right_arr ^ nth) * local_next, local_next, axis=2
+            )
+            if nth:
+                k_now = lax.ppermute(
+                    k_now, axis_id, perm=[(pp, pp ^ nth) for pp in range(view_out)]
+                )
+            z2 = lax.dynamic_update_slice_in_dim(z2, k_now, (right_arr ^ nth) * tile_out, axis=1)
+        return z2
+
+    moved = spread_plane_on(tokens)
     places = moved.shape[2]
     normed = layer_norm(moved, ln_gain).reshape(frames * places, width)
 

time: 152 us -> 132 us (0.87)
  waiting for transfers between devices: 60.1 us -> 29 us
  blocking collectives: 28.2 us -> 35 us
  starting transfers between devices: 7.45 us -> 13.7 us
  local copies, waits for them, and re-layouts: 14.9 us -> 11.9 us
    all_to_all x1 -> x0, waiting for transfers between devices: 58.6 us -> none  [shards(): lax.all_to_all(tokens, 'seq', split_axis=2, concat_axis=1, tiled=True)]
    ppermute x0 -> x7, waiting for transfers between devices: none -> 28.2 us  [spread_plane_on(): lax.ppermute(k_now, axis_id, perm=[(pp, pp ^ nth) for pp in range(view_ou...]
    ppermute x0 -> x7, starting transfers between devices: none -> 13.7 us  [spread_plane_on(): lax.ppermute(k_now, axis_id, perm=[(pp, pp ^ nth) for pp in range(view_ou...]
    all_to_all x1 -> x0, starting transfers between devices: 7.41 us -> none  [shards(): lax.all_to_all(tokens, 'seq', split_axis=2, concat_axis=1, tiled=True)]
    all_to_all x1, blocking collectives: 28.2 us -> 35 us  [shards(): lax.all_to_all(mixed.reshape(1, frames, places, HD), 'seq', split_axis=1,...]
    convert_element_type x1 -> x0, local copies, waits for them, and re-layouts: 2.42 us -> none  [layer_norm(): values = block.astype(jnp.float32)]
    convert_element_type x1 -> x0, other arithmetic: 2.34 us -> none  [layer_norm(): values = block.astype(jnp.float32)]
    unnamed x7 -> x8, local copies, waits for them, and re-layouts: 4.77 us -> 2.74 us
  transfers between devices with their start and end apart: 3 -> 9, of which waited for: 1 -> 4; matrix products, arithmetic and copies ran while one was open for 25% -> 25% of each run, Pallas kernels for 0% -> 0%
where the time goes in v1:
time: 132 us; the launch traced here: 131 us
  blocking collectives  35 us (27%)
  waiting for transfers between devices  29 us (22%)
  matrix products  23.4 us (18%)
  starting transfers between devices  13.7 us (10%)
  between operations  13.6 us (10%)
  local copies, waits for them, and re-layouts  11.9 us (9%)
  other arithmetic  4.72 us (4%)
    all_to_all x1, blocking collectives, shards(): lax.all_to_all(mixed.reshape(1, frames, places, HD), 'seq', split_axis=1,...  35 us
    ppermute x7, waiting for transfers between devices, spread_plane_on(): lax.ppermute(k_now, axis_id, perm=[(pp, pp ^ nth) for pp in range(view_ou...  28.2 us
    ppermute x7, starting transfers between devices, spread_plane_on(): lax.ppermute(k_now, axis_id, perm=[(pp, pp ^ nth) for pp in range(view_ou...  13.7 us
    dot_general x1, matrix products, column_block(): return jnp.dot(normed, piece, preferred_element_type=jnp.float32)  9.89 us
    dot_general x1, matrix products, attend(): jnp.einsum('flhe,glhe->lhfg', queries, keys, preferred_element_type=jnp.f...  5.66 us
    dot_general x1, matrix products, column_block(): return jnp.dot(rows_in, piece, preferred_element_type=jnp.float32)  4.43 us
    dot_general x1, matrix products, attend(): jnp.einsum('lhfg,glhe->flhe', attn_probs, values, preferred_element_type=...  3.41 us
    unnamed x8, local copies, waits for them, and re-layouts  2.74 us
  transfers between devices with their start and end apart: 9, of which 4 were waited for; matrix products, arithmetic and copies ran while one was open for 25% of the time, Pallas kernels for 0%

profile of v1, /device:TPU:0, one launch (start us, length us, event | category | flops | bytes accessed | tf_op | source)
XLA Modules:
  0.0 131.5 jit_solution(11793684833606108414)
XLA Ops:
  6.5 0.7 all-gather.3.cloned.1.call-update
  7.4 0.2 broadcast_in_dim.14
  7.6 1.3 %copy-done = bf16[1,3,256,1280]{3,2,1,0:T(8,128)(2,1)S(1)} copy-done((bf16[1,3,256,1280]{3,2,1,0:T(8,128)(2,1)S(1)}, bf16[1,3,256,1280]{3,2,1,0:T(8,128)(2,1)}, u32[]{:S(2)}) %copy-start) | copy-done | bytes 1966104
  8.9 1.1 constant_dynamic-slice_fusion
  10.0 3.0 %collective-permute-start = (bf16[1,3,32,1280]{3,2,1,0:T(8,128)(2,1)}, bf16[1,3,32,1280]{3,2,1,0:T(8,128)(2,1)S(1)}, u32[]{:S(2)}, u32[]{:S(2)}) collective-permute-start(bf16[1,3,32,1280]{3,2,1,0:T(8,128)(2,1)} %get-tuple-element.12), channel_id=1, source_target_pairs={{0,1},{1,0},{2,3},{3,2},{4,5},{5,4},{6,7},{7,6},{8,9},{9,8},{10,11... | collective-permute-start | bytes 737288 | tf_op jit(solution)/shard_map/ppermute | solution.py:60
  13.0 1.6 %collective-permute-start.1 = (bf16[1,3,32,1280]{3,2,1,0:T(8,128)(2,1)}, bf16[1,3,32,1280]{3,2,1,0:T(8,128)(2,1)S(1)}, u32[]{:S(2)}, u32[]{:S(2)}) collective-permute-start(bf16[1,3,32,1280]{3,2,1,0:T(8,128)(2,1)} %get-tuple-element.11), channel_id=1, source_target_pairs={{0,2},{1,3},{2,0},{3,1},{4,6},{5,7},{6,4},{7,5},{8,10},{9,11},{10,... | collective-permute-start | bytes 737288 | tf_op jit(solution)/shard_map/ppermute | solution.py:60
  14.6 3.0 %collective-permute-start.3 = (bf16[1,3,32,1280]{3,2,1,0:T(8,128)(2,1)}, bf16[1,3,32,1280]{3,2,1,0:T(8,128)(2,1)S(1)}, u32[]{:S(2)}, u32[]{:S(2)}) collective-permute-start(bf16[1,3,32,1280]{3,2,1,0:T(8,128)(2,1)} %get-tuple-element.9), channel_id=1, source_target_pairs={{0,4},{1,5},{2,6},{3,7},{4,0},{5,1},{6,2},{7,3},{8,12},{9,13},{10,... | collective-permute-start | bytes 737288 | tf_op jit(solution)/shard_map/ppermute | solution.py:60
  17.6 1.3 collective-permute-start.4
  18.9 0.1 broadcast_compare_fusion
  18.9 0.2 collective-permute-done
  19.1 3.9 %collective-permute-start.5 = (bf16[1,3,32,1280]{3,2,1,0:T(8,128)(2,1)}, bf16[1,3,32,1280]{3,2,1,0:T(8,128)(2,1)S(1)}, u32[]{:S(2)}, u32[]{:S(2)}) collective-permute-start(bf16[1,3,32,1280]{3,2,1,0:T(8,128)(2,1)} %get-tuple-element.14), channel_id=1, source_target_pairs={{0,6},{1,7},{2,4},{3,5},{4,2},{5,3},{6,0},{7,1},{8,14},{9,15},{10,... | collective-permute-start | bytes 737288 | tf_op jit(solution)/shard_map/ppermute | solution.py:60
  23.0 8.6 %collective-permute-done.1 = bf16[1,3,32,1280]{3,2,1,0:T(8,128)(2,1)S(1)} collective-permute-done((bf16[1,3,32,1280]{3,2,1,0:T(8,128)(2,1)}, bf16[1,3,32,1280]{3,2,1,0:T(8,128)(2,1)S(1)}, u32[]{:S(2)}, u32[]{:S(2)}) %collective-permute-start.1) | collective-permute-done | bytes 245792 | tf_op jit(solution)/shard_map/ppermute | solution.py:60
  31.6 1.0 collective-permute-start.6
  32.7 2.0 %collective-permute-done.2 = bf16[1,3,32,1280]{3,2,1,0:T(8,128)(2,1)S(1)} collective-permute-done((bf16[1,3,32,1280]{3,2,1,0:T(8,128)(2,1)}, bf16[1,3,32,1280]{3,2,1,0:T(8,128)(2,1)S(1)}, u32[]{:S(2)}, u32[]{:S(2)}) %collective-permute-start.2) | collective-permute-done | bytes 245792 | tf_op jit(solution)/shard_map/ppermute | solution.py:60
  34.7 17.5 %collective-permute-done.4 = bf16[1,3,32,1280]{3,2,1,0:T(8,128)(2,1)S(1)} collective-permute-done((bf16[1,3,32,1280]{3,2,1,0:T(8,128)(2,1)}, bf16[1,3,32,1280]{3,2,1,0:T(8,128)(2,1)S(1)}, u32[]{:S(2)}, u32[]{:S(2)}) %collective-permute-start.4) | collective-permute-done | bytes 245792 | tf_op jit(solution)/shard_map/ppermute | solution.py:60
  52.3 0.3 convert_reduce_fusion
  52.6 0.7 fusion.2
  53.3 1.9 %fusion.4 = bf16[1,24,32,1280]{3,2,1,0:T(8,128)(2,1)} fusion(bf16[1,24,32,1280]{3,2,1,0:T(8,128)(2,1)S(1)} %constant_dynamic-update-slice_fusion.6, f32[1280]{0:T(1024)S(1)} %copy-done.2, f32[24,32]{1,0:T(8,128)S(1)} %add_rsqrt_fusion, f32[24,32]{1,0:T(8,128)S(1)} %broadcast_multiply_fusion), kind=kLoop, calls=%fused_computation.7 | loop fusion | flops 4915200 | bytes 3943424 | tf_op jit(solution)/shard_map/convert_element_type | solution.py:17
  55.2 9.9 %fusion.19 = (bf16[768,1920]{1,0:T(8,128)(2,1)S(1)}, f32[768,1920]{1,0:T(8,128)}) fusion(bf16[768,1280]{1,0:T(8,128)(2,1)} %bitcast.21, bf16[1280,1920]{0,1:T(8,128)(2,1)} %all-gather.3.cloned.1.call-done), kind=kOutput, calls=%fused_computation.42 | convolution fusion | flops 3776348160 | bytes 15728640 | tf_op jit(solution)/shard_map/dot_general | solution.py:71
  65.1 0.2 fusion.18
  65.3 1.8 %reshape.55 = bf16[24,32,8,80]{3,2,1,0:T(8,128)(2,1)S(1)} reshape(bf16[768,640]{1,0:T(8,128)(2,1)S(1)} %get-tuple-element.6) | data formatting | bytes 1966080 | tf_op jit(solution)/shard_map/reshape | solution.py:78
  67.1 1.7 %fusion.7 = bf16[768,640]{1,0:T(8,128)(2,1)S(1)} fusion(f32[768,1920]{1,0:T(8,128)} %get-tuple-element.16), kind=kLoop, calls=%fused_computation.13 | loop fusion | flops 983040 | bytes 2949120 | tf_op jit(solution)/shard_map/convert_element_type | solution.py:21
  68.8 2.5 %reshape.54 = bf16[24,32,8,80]{3,2,1,0:T(8,128)(2,1)} reshape(bf16[768,640]{1,0:T(8,128)(2,1)S(1)} %fusion.7) | data formatting | bytes 1966080 | tf_op jit(solution)/shard_map/reshape | solution.py:78
  71.3 5.7 %fusion.6 = (f32[32,8,24]{2,1,0:T(8,128)S(1)}, f32[32,8,24,24]{2,3,1,0:T(8,128)}) fusion(pred[24,24]{0,1:T(8,128)(4,1)S(1)} %broadcast_compare_fusion, bf16[24,32,8,80]{3,2,1,0:T(8,128)(2,1)S(1)} %reshape.55, bf16[24,32,8,80]{3,2,1,0:T(8,128)(2,1)} %reshape.54), kind=kOutput, calls=%fused_computation.11 | convolution fusion | flops 23881728 | bytes 2581056 | tf_op jit(solution)/shard_map/flhe,glhe->lhfg/dot_general | solution.py:28
  77.0 1.6 %reshape.53 = bf16[24,32,8,80]{3,2,1,0:T(8,128)(2,1)S(1)} reshape(bf16[768,640]{1,0:T(8,128)(2,1)S(1)} %get-tuple-element.5) | data formatting | bytes 1966080 | tf_op jit(solution)/shard_map/reshape | solution.py:78
  78.6 3.4 %fusion.14 = bf16[24,32,8,80]{3,0,2,1:T(8,128)(2,1)S(1)} fusion(f32[32,8,24,24]{2,3,1,0:T(8,128)} %get-tuple-element.18, f32[32,8,24]{2,1,0:T(8,128)S(1)} %get-tuple-element.17, pred[24,24]{0,1:T(8,128)(4,1)S(1)} %broadcast_compare_fusion, bf16[24,32,8,80]{3,2,1,0:T(8,128)(2,1)S(1)} %reshape.53), kind=kOutput, calls=%fused_computation.21 | convolution fusion | flops 24526848 | bytes 2581056 | tf_op jit(solution)/shard_map/lhfg,glhe->flhe/dot_general | solution.py:32
  82.0 0.3 copy.26
  82.4 1.2 reshape.56
  83.6 35.0 %all_to_all.15 = bf16[1,24,32,640]{3,2,0,1:T(8,128)(2,1)S(1)} all-to-all(bf16[1,24,32,640]{3,2,0,1:T(8,128)(2,1)S(1)} %bitcast.18), channel_id=1, replica_groups=mesh['dp'=4,'seq'=8] {'seq'}, dimensions={1} | all-to-all | bytes 1966080 | tf_op jit(solution)/shard_map/all_to_all | solution.py:80
  118.6 0.1 copy.28
  118.8 1.4 %copy-done.1 = bf16[1,3,256,1280]{3,2,1,0:T(8,128)(2,1)S(1)} copy-done((bf16[1,3,256,1280]{3,2,1,0:T(8,128)(2,1)S(1)}, bf16[1,3,256,1280]{3,2,1,0:T(8,128)(2,1)}, u32[]{:S(2)}) %copy-start.1) | copy-done | bytes 1966104
  120.2 4.4 %fusion.5 = bf16[768,1280]{1,0:T(8,128)(2,1)} fusion(bf16[768,640]{1,0:T(8,128)(2,1)S(1)} %bitcast.22, bf16[640,1280]{0,1:T(8,128)(2,1)} %all-gather.5.cloned.1.call-done, bf16[768,1280]{1,0:T(8,128)(2,1)S(1)} %bitcast.20), kind=kOutput, calls=%fused_computation.8 | convolution fusion | flops 1261240320 | bytes 6553600 | tf_op jit(solution)/shard_map/dot_general | solution.py:87
  (24 shorter events, 0.3 us)
Async XLA Ops:
  6.5 48.7 %all-gather.3.cloned.1.call-start = ((), (), s32[]{:S(2)}) async-start(), calls=%async_computation.1 | async-start | bytes 6144000 | tf_op jit(solution)/shard_map/all_gather | solution.py:74
  7.3 111.5 %all-gather.5.cloned.1.call-start = ((), (), s32[]{:S(2)}) async-start(), calls=%async_computation.2 | async-start | bytes 2048000 | tf_op jit(solution)/shard_map/all_gather | solution.py:89
  7.3 1.5 %copy-start = (bf16[1,3,256,1280]{3,2,1,0:T(8,128)(2,1)S(1)}, bf16[1,3,256,1280]{3,2,1,0:T(8,128)(2,1)}, u32[]{:S(2)}) copy-start(bf16[1,3,256,1280]{3,2,1,0:T(8,128)(2,1)} %param.5) | copy-start | bytes 5898244
  8.9 10.0 %copy-start.3 = (s32[1,24]{1,0:T(1,128)S(1)}, s32[1,24]{1,0:T(1,128)}, u32[]{:S(2)}) copy-start(s32[1,24]{1,0:T(1,128)} %param.6) | copy-start | bytes 292
  10.0 9.1 %collective-permute-start = (bf16[1,3,32,1280]{3,2,1,0:T(8,128)(2,1)}, bf16[1,3,32,1280]{3,2,1,0:T(8,128)(2,1)S(1)}, u32[]{:S(2)}, u32[]{:S(2)}) collective-permute-start(bf16[1,3,32,1280]{3,2,1,0:T(8,128)(2,1)} %get-tuple-element.12), channel_id=1, source_target_pairs={{0,1},{1,0},{2,3},{3,2},{4,5},{5,4},{6,7},{7,6},{8,9},{9,8},{10,11... | collective-permute-start | bytes 737288 | tf_op jit(solution)/shard_map/ppermute | solution.py:60
  13.0 18.6 %collective-permute-start.1 = (bf16[1,3,32,1280]{3,2,1,0:T(8,128)(2,1)}, bf16[1,3,32,1280]{3,2,1,0:T(8,128)(2,1)S(1)}, u32[]{:S(2)}, u32[]{:S(2)}) collective-permute-start(bf16[1,3,32,1280]{3,2,1,0:T(8,128)(2,1)} %get-tuple-element.11), channel_id=1, source_target_pairs={{0,2},{1,3},{2,0},{3,1},{4,6},{5,7},{6,4},{7,5},{8,10},{9,11},{10,... | collective-permute-start | bytes 737288 | tf_op jit(solution)/shard_map/ppermute | solution.py:60
  14.6 20.1 %collective-permute-start.2 = (bf16[1,3,32,1280]{3,2,1,0:T(8,128)(2,1)}, bf16[1,3,32,1280]{3,2,1,0:T(8,128)(2,1)S(1)}, u32[]{:S(2)}, u32[]{:S(2)}) collective-permute-start(bf16[1,3,32,1280]{3,2,1,0:T(8,128)(2,1)} %get-tuple-element.10), channel_id=1, source_target_pairs={{0,3},{1,2},{2,1},{3,0},{4,7},{5,6},{6,5},{7,4},{8,11},{9,10},{10,... | collective-permute-start | bytes 737288 | tf_op jit(solution)/shard_map/ppermute | solution.py:60
  14.6 20.1 %collective-permute-start.3 = (bf16[1,3,32,1280]{3,2,1,0:T(8,128)(2,1)}, bf16[1,3,32,1280]{3,2,1,0:T(8,128)(2,1)S(1)}, u32[]{:S(2)}, u32[]{:S(2)}) collective-permute-start(bf16[1,3,32,1280]{3,2,1,0:T(8,128)(2,1)} %get-tuple-element.9), channel_id=1, source_target_pairs={{0,4},{1,5},{2,6},{3,7},{4,0},{5,1},{6,2},{7,3},{8,12},{9,13},{10,... | collective-permute-start | bytes 737288 | tf_op jit(solution)/shard_map/ppermute | solution.py:60
  17.6 34.6 %collective-permute-start.4 = (bf16[1,3,32,1280]{3,2,1,0:T(8,128)(2,1)}, bf16[1,3,32,1280]{3,2,1,0:T(8,128)(2,1)S(1)}, u32[]{:S(2)}, u32[]{:S(2)}) collective-permute-start(bf16[1,3,32,1280]{3,2,1,0:T(8,128)(2,1)} %get-tuple-element.8), channel_id=1, source_target_pairs={{0,5},{1,4},{2,7},{3,6},{4,1},{5,0},{6,3},{7,2},{8,13},{9,12},{10,... | collective-permute-start | bytes 737288 | tf_op jit(solution)/shard_map/ppermute | solution.py:60
  19.1 33.1 %collective-permute-start.5 = (bf16[1,3,32,1280]{3,2,1,0:T(8,128)(2,1)}, bf16[1,3,32,1280]{3,2,1,0:T(8,128)(2,1)S(1)}, u32[]{:S(2)}, u32[]{:S(2)}) collective-permute-start(bf16[1,3,32,1280]{3,2,1,0:T(8,128)(2,1)} %get-tuple-element.14), channel_id=1, source_target_pairs={{0,6},{1,7},{2,4},{3,5},{4,2},{5,3},{6,0},{7,1},{8,14},{9,15},{10,... | collective-permute-start | bytes 737288 | tf_op jit(solution)/shard_map/ppermute | solution.py:60
  31.6 20.6 %collective-permute-start.6 = (bf16[1,3,32,1280]{3,2,1,0:T(8,128)(2,1)S(1)}, bf16[1,3,32,1280]{3,2,1,0:T(8,128)(2,1)S(1)}, u32[]{:S(2)}, u32[]{:S(2)}) collective-permute-start(bf16[1,3,32,1280]{3,2,1,0:T(8,128)(2,1)S(1)} %get-tuple-element.7), channel_id=1, source_target_pairs={{0,7},{1,6},{2,5},{3,4},{4,3},{5,2},{6,1},{7,0},{8,15},{9,14},{10,... | collective-permute-start | bytes 737288 | tf_op jit(solution)/shard_map/ppermute | solution.py:60
  52.3 1.0 copy-start.2
  118.6 1.5 %copy-start.1 = (bf16[1,3,256,1280]{3,2,1,0:T(8,128)(2,1)S(1)}, bf16[1,3,256,1280]{3,2,1,0:T(8,128)(2,1)}, u32[]{:S(2)}) copy-start(bf16[1,3,256,1280]{3,2,1,0:T(8,128)(2,1)} %param.5) | copy-start | bytes 5898244
Sparse Core Ops, SparseCore 0:
  8.9 41.2 all-gather.2
  51.8 19.9 all-gather.4
